TPU v7x, 128 devices: a whole 4x4x4 slice. The times are simulated.
128 devices in a mesh: layer: 4 (over x_hi, core), feat: 16 (over z, y), par: 2 (over x_lo).
Axes of the slice: x: 4 (x_hi: 2, x_lo: 2; x = x_hi * 2 + x_lo), y: 4, z: 4, core: 2. Of those that a mesh axis runs over, the one named last changes fastest.
Arguments:
- residual: bfloat16 [4, 512, 2304], P('layer'), may hold values from -6 to 6
- norm_gain: float32 [4, 2304], P('layer'), may hold values from 0.5 to 1.5
- gate_weight: bfloat16 [4, 2304, 9216], P('layer', None, ('feat', 'par')), may hold values from -0.125 to 0.125
- up_weight: bfloat16 [4, 2304, 9216], P('layer', None, ('feat', 'par')), may hold values from -0.125 to 0.125
- down_weight: bfloat16 [4, 9216, 2304], P('layer', ('feat', 'par')), may hold values from -0.0625 to 0.0625
- enc_weight: float32 [4, 2304, 8192], P('layer', 'par', 'feat'), may hold values from -0.125 to 0.125
- enc_bias: float32 [4, 8192], P('layer', 'feat'), may hold values from -1 to 0.5
- dec_weight: bfloat16 [4, 2, 2, 8192, 2304], P('layer', 'par', None, 'feat'), may hold values from -0.0625 to 0.0625
- dec_bias: float32 [4, 2304], replicated, may hold values from -3 to 3
Outputs:
- enc_grad: float32 [4, 2304, 8192], P('layer', 'par', 'feat')
- enc_bias_grad: float32 [4, 8192], P('layer', 'feat')
- dec_grad: bfloat16 [4, 2, 2, 8192, 2304], P('layer', 'par', None, 'feat')
All inputs are finite; a program needn't handle non-finite values.
Results may differ from a plain program's by a relative error of at most 0.007.
Values may be sent and summed in bfloat16 or wider, within the bound.
A program may use at most 192 MiB of HBM per device.

v0:
```python
import jax
import jax.numpy as jnp
from jax import lax
from jax.sharding import PartitionSpec as P


def rms_normed(rows_in, gain_row):
    values = rows_in.astype(jnp.float32)
    scaling = lax.rsqrt(jnp.mean(values * values, axis=-1, keepdims=True) + 1e-06)
    return (values * scaling * gain_row).astype(jnp.bfloat16)


def shards(
    residual,
    norm_gain,
    gate_weight,
    up_weight,
    down_weight,
    enc_weight,
    enc_bias,
    dec_weight,
    dec_bias,
):
    highest = lax.Precision.HIGHEST
    source = lax.axis_index("layer")
    parity = lax.axis_index("par")
    slot_count = dec_weight.shape[2]
    normed = rms_normed(residual[0], norm_gain[0])
    tokens, model_width = normed.shape
    gate_value = jnp.dot(normed, gate_weight[0], preferred_element_type=jnp.float32)
    up_value = jnp.dot(normed, up_weight[0], preferred_element_type=jnp.float32)
    hidden = (jax.nn.gelu(gate_value, approximate=True) * up_value).astype(jnp.bfloat16)
    target_part = jnp.dot(hidden, down_weight[0], preferred_element_type=jnp.float32)
    half_width = enc_weight.shape[1]
    my_rows = lax.dynamic_slice_in_dim(normed, parity * half_width, half_width, 1).astype(
        jnp.float32
    )
    pre_part = jnp.dot(my_rows, enc_weight[0], precision=highest)
    pre_act = lax.psum(pre_part, "par") + enc_bias[0]
    positive = jnp.maximum(pre_act, 0.0)
    actives = (positive * positive).astype(jnp.bfloat16)
    slot_ids = jnp.arange(slot_count, dtype=jnp.int32)
    slot_live = 2 * slot_ids + parity >= source
    live_float = slot_live.astype(jnp.float32)
    decoders = dec_weight[0, 0]
    recon_parts = (
        jnp.einsum("tf,jfd->jtd", actives, decoders, preferred_element_type=jnp.float32)
        * live_float[:, None, None]
    )
    bias_slots = lax.dynamic_index_in_dim(
        dec_bias.reshape(slot_count, 2, model_width), parity, 1, keepdims=False
    )
    full_target = lax.psum(target_part, ("feat", "par"))
    all_targets = lax.all_gather(full_target[None], "layer", axis=0, tiled=True)
    target_slots = lax.dynamic_index_in_dim(
        all_targets.reshape(slot_count, 2, tokens, model_width), parity, 1, keepdims=False
    )
    summed_rows = lax.psum(recon_parts, ("layer", "feat"))
    err_full = summed_rows + bias_slots[:, None, :]
    err_full = err_full - target_slots
    errors = (err_full * 0.0625).astype(jnp.bfloat16)
    masked = errors * slot_live.astype(jnp.bfloat16)[:, None, None]
    back_part = jnp.einsum("jtd,jfd->tf", masked, decoders, preferred_element_type=jnp.float32)
    back_grad = lax.psum(back_part.astype(jnp.bfloat16), "par").astype(jnp.float32)
    d_pre = back_grad * 2.0 * positive
    enc_grad = lax.dot_general(my_rows, d_pre, (((0,), (0,)), ((), ())), precision=highest)
    bias_grad = jnp.sum(d_pre, axis=0)
    dec_grad = jnp.einsum(
        "tf,jtd->jfd", actives, masked, preferred_element_type=jnp.float32
    ).astype(jnp.bfloat16)
    return (enc_grad[None], bias_grad[None], dec_grad[None, None])


def solution(mesh):
    return jax.shard_map(
        shards,
        mesh=mesh,
        in_specs=(
            P("layer", None, None),
            P("layer", None),
            P("layer", None, ("feat", "par")),
            P("layer", None, ("feat", "par")),
            P("layer", ("feat", "par"), None),
            P("layer", "par", "feat"),
            P("layer", "feat"),
            P("layer", "par", None, "feat", None),
            P(),
        ),
        out_specs=(
            P("layer", "par", "feat"),
            P("layer", "feat"),
            P("layer", "par", None, "feat", None),
        ),
        check_vma=False,
    )
```

profile of v0, /device:TPU:1, one launch (start us, length us, event | category | flops | bytes accessed | tf_op | source)
XLA Modules:
  0.0 1276.6 jit_solution(10719600831375024537)
XLA Ops:
  7.2 0.0 all-reduce.5.cloned.1.call-start
  7.2 2.4 multiply_reduce_fusion
  9.6 4.2 convert_bitcast_fusion
  13.8 0.1 dynamic-slice
  13.9 4.9 fusion.12
  18.9 0.0 all-reduce.9.cloned.1.call-start
  18.9 3.2 fusion.43
  22.2 6.3 convolution_bitcast_fusion
  28.4 0.0 all-reduce.9.cloned.1.call-update
  28.5 0.0 all-reduce.7.cloned.1.call-start
  28.5 40.3 %all-reduce.5.cloned.1.call-done = f32[512,512]{1,0:T(8,128)} async-done(((f32[512,512]{1,0:T(8,128)}), f32[512,512]{1,0:T(8,128)}) %all-reduce.5.cloned.1.call-update) | async-done | bytes 1048592 | tf_op jit(solution)/shard_map/psum | solution.py:39
  68.8 8.9 multiply_bitcast_fusion
  77.8 0.0 all-gather.2.cloned.1.call-start
  77.8 314.6 %all-reduce.9.cloned.1.call-done = f32[1,512,2304]{2,1,0:T(8,128)} async-done(((f32[1,512,2304]{2,1,0:T(8,128)}), f32[1,512,2304]{2,1,0:T(8,128)}) %all-reduce.9.cloned.1.call-update) | async-done | bytes 4718608 | tf_op jit(solution)/shard_map/psum | solution.py:53
  392.5 0.2 all-reduce.11.cloned.1.call-start
  392.8 668.2 %all-reduce.7.cloned.1.call-done = f32[2,512,2304]{2,1,0:T(8,128)} async-done(((f32[2,512,2304]{2,1,0:T(8,128)}), f32[2,512,2304]{2,1,0:T(8,128)}) %all-reduce.7.cloned.1.call-update) | async-done | bytes 9437200 | tf_op jit(solution)/shard_map/psum | solution.py:58
  1061.0 149.9 %all-gather.2.cloned.1.call-done = f32[4,512,2304]{2,1,0:T(8,128)} async-done(((f32[1,512,2304]{2,1,0:T(8,128)}), f32[4,512,2304]{2,1,0:T(8,128)}) %all-gather.2.cloned.1.call-update) | async-done | bytes 18874384 | tf_op jit(solution)/shard_map/all_gather | solution.py:54
  1210.8 10.1 fusion.5
  1220.9 7.3 fusion.22
  1228.2 6.7 fusion.2
  1234.9 6.8 copy.17
  1241.7 21.0 %all-reduce.11.cloned.1.call-done = bf16[512,512]{1,0:T(8,128)(2,1)} async-done(((bf16[512,512]{1,0:T(8,128)(2,1)}), bf16[512,512]{1,0:T(8,128)(2,1)}) %all-reduce.11.cloned.1.call-update) | async-done | bytes 524304 | tf_op jit(solution)/shard_map/psum | solution.py:64
  1262.7 1.8 fusion.48
  1264.6 5.5 convolution_bitcast_fusion.1
  (25 shorter events, 0.2 us)
Async XLA Ops:
  7.2 6.7 copy-start
  7.2 61.7 %all-reduce.5.cloned.1.call-start = ((), (), s32[]{:S(2)}) async-start(), calls=%async_computation | async-start | bytes 2097152 | tf_op jit(solution)/shard_map/psum | solution.py:39
  7.2 6.5 copy-start.6
  18.9 3.3 copy-start.2
  18.9 373.6 %all-reduce.9.cloned.1.call-start = ((), (), s32[]{:S(2)}) async-start(), calls=%async_computation.2 | async-start | bytes 9437184 | tf_op jit(solution)/shard_map/psum | solution.py:53
  28.4 40.4 %copy-start.5 = (f32[1,512]{1,0:T(1,128)S(1)}, f32[1,512]{1,0:T(1,128)}, u32[]{:S(2)}) copy-start(f32[1,512]{1,0:T(1,128)} %param.15) | copy-start | bytes 6148
  28.5 1032.5 %all-reduce.7.cloned.1.call-start = ((), (), s32[]{:S(2)}) async-start(), calls=%async_computation.1 | async-start | bytes 18874368 | tf_op jit(solution)/shard_map/psum | solution.py:58
  77.8 314.9 %copy-start.4 = (f32[4,2304]{1,0:T(4,128)S(1)}, f32[4,2304]{1,0:T(4,128)}, u32[]{:S(2)}) copy-start(f32[4,2304]{1,0:T(4,128)} %param.17) | copy-start | bytes 110596
  77.8 1133.0 %all-gather.2.cloned.1.call-start = ((), (), s32[]{:S(2)}) async-start(), calls=%async_computation.3 | async-start | bytes 23592960 | tf_op jit(solution)/shard_map/all_gather | solution.py:54
  392.5 870.3 %all-reduce.11.cloned.1.call-start = ((), (), s32[]{:S(2)}) async-start(), calls=%async_computation.4 | async-start | bytes 1048576 | tf_op jit(solution)/shard_map/psum | solution.py:64
  1220.9 7.3 copy-start.3
  1234.9 35.2 %copy-start.1 = (f32[1,1152,512]{2,1,0:T(8,128)S(1)}, f32[1,1152,512]{2,1,0:T(8,128)}, u32[]{:S(2)}) copy-start(f32[1,1152,512]{2,1,0:T(8,128)} %param.14) | copy-start | bytes 7077892
Sparse Core Ops, SparseCore 0:
  19.0 49.8 all-reduce.4
  72.1 320.3 all-reduce.8
  395.1 665.8 all-reduce.6
  1062.6 148.1 all-gather.1
  1228.3 34.3 all-reduce.10
where the time goes:
time: 1280 us
  waiting for transfers between devices  1190 us (93%)
  matrix products  42.9 us (3%)
  other arithmetic  18.5 us (1%)
  between operations  13.9 us (1%)
    psum x1, waiting for transfers between devices, shards(): summed_rows = lax.psum(recon_parts, ('layer', 'feat'))  668 us
    psum x1, waiting for transfers between devices, shards(): full_target = lax.psum(target_part, ('feat', 'par'))  315 us
    all_gather x1, waiting for transfers between devices, shards(): all_targets = lax.all_gather(full_target[None], 'layer', axis=0, tiled=True)  150 us
    psum x1, waiting for transfers between devices, shards(): pre_act = lax.psum(pre_part, 'par') + enc_bias[0]  40.3 us
  transfers between devices with their start and end apart: 5, of which 5 were waited for; matrix products, arithmetic and copies ran while one was open for 3% of the time, Pallas kernels for 0%

commit v1 on v0

--- a/solution.py
+++ b/solution.py
@@ -1,7 +1,17 @@
+import functools
 import jax
 import jax.numpy as jnp
 from jax import lax
 from jax.sharding import PartitionSpec as P
+from jax.lax import psum
+
+
+def _form_core(v0, row_axis, net_axis):
+    everything = psum(psum(v0, axis_name=row_axis), axis_name=net_axis)
+    return everything
+
+
+_do_tables = functools.partial(_form_core, row_axis="par", net_axis="feat")
 
 
 def rms_normed(rows_in, gain_row):
@@ -50,7 +60,7 @@
     bias_slots = lax.dynamic_index_in_dim(
         dec_bias.reshape(slot_count, 2, model_width), parity, 1, keepdims=False
     )
-    full_target = lax.psum(target_part, ("feat", "par"))
+    full_target = _do_tables(target_part)
     all_targets = lax.all_gather(full_target[None], "layer", axis=0, tiled=True)
     target_slots = lax.dynamic_index_in_dim(
         all_targets.reshape(slot_count, 2, tokens, model_width), parity, 1, keepdims=False

time: 1280 us -> 1160 us (0.906)
  waiting for transfers between devices: 1190 us -> 1080 us
    psum x2, waiting for transfers between devices: 355 us -> 257 us  [_form_core(): everything = psum(psum(v0, axis_name=row_axis), axis_name=net_axis)]
    psum x1, waiting for transfers between devices: 668 us -> 648 us  [shards(): summed_rows = lax.psum(recon_parts, ('layer', 'feat'))]
  transfers between devices with their start and end apart: 5 -> 5, of which waited for: 5 -> 5; matrix products, arithmetic and copies ran while one was open for 3% -> 2% of each run, Pallas kernels for 0% -> 0%
where the time goes in v1:
time: 1160 us
  waiting for transfers between devices  1080 us (93%)
  matrix products  40.4 us (3%)
  other arithmetic  18.5 us (2%)
  between operations  13.9 us (1%)
    psum x1, waiting for transfers between devices, shards(): summed_rows = lax.psum(recon_parts, ('layer', 'feat'))  648 us
    psum x2, waiting for transfers between devices, _form_core(): everything = psum(psum(v0, axis_name=row_axis), axis_name=net_axis)  257 us
    all_gather x1, waiting for transfers between devices, shards(): all_targets = lax.all_gather(full_target[None], 'layer', axis=0, tiled=True)  150 us
  transfers between devices with their start and end apart: 5, of which 5 were waited for; matrix products, arithmetic and copies ran while one was open for 2% of the time, Pallas kernels for 0%

profile of v1, /device:TPU:1, one launch (start us, length us, event | category | flops | bytes accessed | tf_op | source)
XLA Modules:
  0.0 1156.4 jit_solution(8377540999475604657)
XLA Ops:
  7.2 2.4 multiply_reduce_fusion
  9.6 4.2 convert_bitcast_fusion
  13.8 0.1 dynamic-slice
  13.9 3.2 fusion.43
  17.1 0.2 copy-done.2
  17.3 3.3 fusion.12
  20.6 7.0 fusion.17
  27.6 0.0 all-reduce.8.cloned.1.call-start
  27.7 152.1 %all-reduce.12.cloned.1.call-done = (f32[512,2304]{1,0:T(8,128)}, f32[512,512]{1,0:T(8,128)}) async-done(((f32[512,2304]{1,0:T(8,128)}, f32[512,512]{1,0:T(8,128)}), (f32[512,2304]{1,0:T(8,128)}, f32[512,512]{1,0:T(8,128)})) %all-reduce.12.cloned.1.call-update) | async-done | bytes 5767184 | tf_op jit(solution)/shard_map/psum | solution.py:10
  179.8 0.0 all-reduce.6.cloned.1.call-start
  179.9 1.1 copy-done.3
  181.0 7.4 multiply_bitcast_fusion
  188.4 0.0 all-gather.2.cloned.1.call-start
  188.5 104.4 %all-reduce.8.cloned.1.call-done = f32[1,512,2304]{2,1,0:T(8,128)} async-done(((f32[1,512,2304]{2,1,0:T(8,128)}), f32[1,512,2304]{2,1,0:T(8,128)}) %all-reduce.8.cloned.1.call-update) | async-done | bytes 4718608 | tf_op jit(solution)/shard_map/psum | solution.py:10
  292.9 0.2 all-reduce.10.cloned.1.call-start
  293.3 647.9 %all-reduce.6.cloned.1.call-done = f32[2,512,2304]{2,1,0:T(8,128)} async-done(((f32[2,512,2304]{2,1,0:T(8,128)}), f32[2,512,2304]{2,1,0:T(8,128)}) %all-reduce.6.cloned.1.call-update) | async-done | bytes 9437200 | tf_op jit(solution)/shard_map/psum | solution.py:68
  941.2 149.5 %all-gather.2.cloned.1.call-done = f32[4,512,2304]{2,1,0:T(8,128)} async-done(((f32[1,512,2304]{2,1,0:T(8,128)}), f32[4,512,2304]{2,1,0:T(8,128)}) %all-gather.2.cloned.1.call-update) | async-done | bytes 18874384 | tf_op jit(solution)/shard_map/all_gather | solution.py:64
  1090.7 10.1 fusion.5
  1100.8 7.2 fusion.23
  1108.0 6.7 fusion.2
  1114.7 6.8 copy.17
  1121.5 21.0 %all-reduce.10.cloned.1.call-done = bf16[512,512]{1,0:T(8,128)(2,1)} async-done(((bf16[512,512]{1,0:T(8,128)(2,1)}), bf16[512,512]{1,0:T(8,128)(2,1)}) %all-reduce.10.cloned.1.call-update) | async-done | bytes 524304 | tf_op jit(solution)/shard_map/psum | solution.py:74
  1142.5 1.8 fusion.48
  1144.3 5.5 convolution_bitcast_fusion
  (25 shorter events, 0.3 us)
Async XLA Ops:
  7.2 10.0 copy-start
  7.2 172.6 %all-reduce.12.cloned.1.call-start = ((), (), s32[]{:S(2)}) async-start(), calls=%async_computation.4 | async-start | bytes 11534336 | tf_op jit(solution)/shard_map/psum | solution.py:10
  7.2 6.5 copy-start.6
  13.9 3.4 copy-start.2
  27.6 152.3 %copy-start.5 = (f32[1,512]{1,0:T(1,128)S(1)}, f32[1,512]{1,0:T(1,128)}, u32[]{:S(2)}) copy-start(f32[1,512]{1,0:T(1,128)} %param.15) | copy-start | bytes 6148
  27.6 265.3 %all-reduce.8.cloned.1.call-start = ((), (), s32[]{:S(2)}) async-start(), calls=%async_computation.1 | async-start | bytes 9437184 | tf_op jit(solution)/shard_map/psum | solution.py:10
  179.8 1.2 copy-start.3
  179.8 761.3 %all-reduce.6.cloned.1.call-start = ((), (), s32[]{:S(2)}) async-start(), calls=%async_computation | async-start | bytes 18874368 | tf_op jit(solution)/shard_map/psum | solution.py:68
  188.4 104.7 %copy-start.4 = (f32[4,2304]{1,0:T(4,128)S(1)}, f32[4,2304]{1,0:T(4,128)}, u32[]{:S(2)}) copy-start(f32[4,2304]{1,0:T(4,128)} %param.17) | copy-start | bytes 110596
  188.4 902.3 %all-gather.2.cloned.1.call-start = ((), (), s32[]{:S(2)}) async-start(), calls=%async_computation.2 | async-start | bytes 23592960 | tf_op jit(solution)/shard_map/all_gather | solution.py:64
  292.9 849.6 %all-reduce.10.cloned.1.call-start = ((), (), s32[]{:S(2)}) async-start(), calls=%async_computation.3 | async-start | bytes 1048576 | tf_op jit(solution)/shard_map/psum | solution.py:74
  1114.7 35.2 %copy-start.1 = (f32[1,1152,512]{2,1,0:T(8,128)S(1)}, f32[1,1152,512]{2,1,0:T(8,128)}, u32[]{:S(2)}) copy-start(f32[1,1152,512]{2,1,0:T(8,128)} %param.14) | copy-start | bytes 7077892
Sparse Core Ops, SparseCore 0:
  27.8 151.9 all-reduce.11
  183.6 109.2 all-reduce.7
  295.4 645.7 all-reduce.5
  942.7 147.9 all-gather.1
  1108.1 34.3 all-reduce.9
